TPU v7x, 32 devices: a whole 2x2x4 slice. The times are simulated.
32 devices in a mesh: mem: 8 (over y, x, core), band: 4 (over z).
Axes of the slice: x: 2, y: 2, z: 4, core: 2. Of those that a mesh axis runs over, the one named last changes fastest.
Arguments:
- ensemble: bfloat16 [256, 3, 240, 160], P('mem', None, 'band'), may hold values from -8 to 8, as said below
- layer_depth: float32 [240, 160], P('band'), may hold values from 0.5 to 2
- observed_cell: int32 [8, 8, 512], P('mem', 'band'), may hold values from 0 to 1799
- observed_value: float32 [8, 8, 512], P('mem', 'band'), may hold values from -6 to 6
- error_variance: float32 [8, 8, 512], P('mem', 'band'), may hold values from 4 to 64
- observed_count: int32 [8, 8], P('mem', 'band'), may hold values from 256 to 512, as said below
Outputs:
- analysis: bfloat16 [256, 3, 240, 160], P('mem', None, 'band')
Inputs may be any that keep to these rules, and one draw needn't show every extreme that they name: `ensemble`: the forecast members scatter around a common state. `observed_count`: some tile holds 512 observations; the slots from the count on are unused.
All inputs are finite; a program needn't handle non-finite values.
Results may differ from a plain program's by a relative error of at most 0.0051.
The roundings to bfloat16 on the way count: a program that leaves them out, or rounds other values in their place, can miss the bound.
Values may be sent and summed in bfloat16 or wider, within the bound.
No kernel may reach another device: no remote copies, remote signals or barrier semaphores. Data moves between devices by JAX's collectives and lax.ppermute only.
A program may use at most 128 MiB of HBM per device.

v0:
```python
import math
import jax
import jax.numpy as jnp
from jax import lax
from jax.sharding import PartitionSpec as P

SWEEPS = 5
half_step = 0.1
coriolis_scale = 0.3
neighbour_weight = 0.75


def padded_2(cells, sides, width):
    for axis, dim in sides:
        count = lax.axis_size(axis)
        head = lax.slice_in_dim(cells, 0, width, axis=dim)
        tail = lax.slice_in_dim(cells, cells.shape[dim] - width, cells.shape[dim], axis=dim)
        cells = jnp.concatenate(
            [
                lax.ppermute(tail, axis, [(i, (i + 1) % count) for i in range(count)]),
                cells,
                lax.ppermute(head, axis, [((i + 1) % count, i) for i in range(count)]),
            ],
            axis=dim,
        )
    return cells


def north_south(source):
    widths = [(0, 0)] * (source.ndim - 1) + [(1, 1)]
    padded = jnp.pad(source, widths)
    return padded[..., 2:] - padded[..., :-2]


def coriolis(latitudes):
    position = jnp.arange(latitudes, dtype=jnp.float32)
    return coriolis_scale * jnp.sin(math.pi * ((position + 0.5) / latitudes - 0.5))


def newton_schulz(starting):
    identity = jnp.eye(starting.shape[-1], dtype=starting.dtype)
    root_part = starting
    inverse_root = jnp.broadcast_to(identity, starting.shape)
    for sweep_index in range(SWEEPS):
        product = jnp.einsum(
            "tij,tjk->tik", inverse_root, root_part, precision=lax.Precision.HIGHEST
        )
        middle = 1.5 * identity - 0.5 * product
        root_part = jnp.einsum("tij,tjk->tik", root_part, middle, precision=lax.Precision.HIGHEST)
        inverse_root = jnp.einsum(
            "tij,tjk->tik", middle, inverse_root, precision=lax.Precision.HIGHEST
        )
    return inverse_root


def on_device(ensemble, layer_depth, observed_cell, observed_value, error_variance, observed_count):
    block_members = ensemble.shape[0]
    columns = ensemble.shape[2]
    latitudes = ensemble.shape[3]
    strips = lax.axis_size("mem")
    members = block_members * strips
    strip_rows = latitudes // strips
    tile_count = observed_cell.shape[1]
    tile_columns = columns // tile_count
    slot_count = observed_cell.shape[2]
    tile_cells = 3 * tile_columns * strip_rows
    height = ensemble[:, 0].astype(jnp.float32)
    eastward = ensemble[:, 1].astype(jnp.float32)
    northward = ensemble[:, 2].astype(jnp.float32)
    turning = coriolis(latitudes)
    flux_east = (layer_depth * eastward).astype(jnp.bfloat16)
    flux_north = (layer_depth * northward).astype(jnp.bfloat16)
    east_margin = padded_2(flux_east, (("band", 1),), 1)
    east_west = east_margin[:, 2:].astype(jnp.float32) - east_margin[:, :-2].astype(jnp.float32)
    north_local = lax.optimization_barrier(flux_north).astype(jnp.float32)
    raised = height - half_step * (east_west + north_south(north_local))
    surface_elevation_cast = raised.astype(jnp.bfloat16)
    height_margin = padded_2(surface_elevation_cast, (("band", 1),), 1)
    margin_wide = height_margin.astype(jnp.float32)
    height_inner = margin_wide[:, 1:-1]
    revised_zonal_velocity = (
        eastward + turning * northward - half_step * (margin_wide[:, 2:] - margin_wide[:, :-2])
    )
    revised_meridional_velocity = (
        northward - turning * eastward - half_step * north_south(height_inner)
    )
    advance_dynamics = jnp.stack(
        [
            surface_elevation_cast,
            revised_zonal_velocity.astype(jnp.bfloat16),
            revised_meridional_velocity.astype(jnp.bfloat16),
        ],
        axis=1,
    )
    reordered = advance_dynamics.reshape(
        block_members, 3, tile_count, tile_columns, strips, strip_rows
    )
    reordered = jnp.transpose(reordered, (4, 2, 0, 1, 3, 5)).reshape(
        strips, tile_count, block_members, tile_cells
    )
    tile_block = lax.all_to_all(reordered, "mem", split_axis=0, concat_axis=2, tiled=True)[0]
    cells_here = observed_cell[0]
    values = jnp.take_along_axis(tile_block, cells_here[:, None, :], axis=2)
    observed_mean = jnp.sum(values, axis=1, dtype=jnp.float32) / members
    slot_index = jnp.arange(slot_count, dtype=jnp.int32)[None, :]
    live_slots = slot_index < observed_count[0][:, None]
    root_weight = jnp.sqrt(jnp.where(live_slots, 1.0 / error_variance[0], 0.0))
    spread = (
        root_weight[:, None, :] * (values.astype(jnp.float32) - observed_mean[:, None, :])
    ).astype(jnp.bfloat16)
    misfit = (root_weight * (observed_value[0] - observed_mean)).astype(jnp.bfloat16)
    spread_margin, misfit_margin = (
        padded_2(spread[None], (("mem", 0), ("band", 1)), 1),
        padded_2(misfit[None], (("mem", 0), ("band", 1)), 1),
    )
    gram_margin = jnp.einsum(
        "atko,atlo->atkl", spread_margin, spread_margin, preferred_element_type=jnp.float32
    )
    pull_margin = jnp.einsum(
        "atko,ato->atk", spread_margin, misfit_margin, preferred_element_type=jnp.float32
    )
    strip_here = lax.axis_index("mem")
    lower_valid = (strip_here > 0).astype(jnp.float32)
    upper_valid = (strip_here < strips - 1).astype(jnp.float32)
    strip_mask = (lower_valid, 1.0, upper_valid)
    total_gram = jnp.zeros((tile_count, members, members), jnp.float32)
    total_pull = jnp.zeros((tile_count, members), jnp.float32)
    for offset_lat in range(3):
        for offset_lon in range(3):
            factor = (
                neighbour_weight ** (abs(offset_lat - 1) + abs(offset_lon - 1))
                * strip_mask[offset_lat]
            )
            total_gram = (
                total_gram + factor * gram_margin[offset_lat, offset_lon : offset_lon + tile_count]
            )
            total_pull = (
                total_pull + factor * pull_margin[offset_lat, offset_lon : offset_lon + tile_count]
            )
    system = (members - 1) * jnp.eye(members, dtype=jnp.float32)[None] + total_gram
    frobenius = jnp.sqrt(jnp.sum(system * system, axis=(1, 2)))
    inverse_root = newton_schulz(system / frobenius[:, None, None])
    spread_map = inverse_root * (math.sqrt(members - 1) / jnp.sqrt(frobenius))[:, None, None]
    half_pull = jnp.einsum("tij,tj->ti", inverse_root, total_pull, precision=lax.Precision.HIGHEST)
    shift_weights = (
        jnp.einsum("tij,tj->ti", inverse_root, half_pull, precision=lax.Precision.HIGHEST)
        / frobenius[:, None]
    )
    weights = (spread_map + shift_weights[:, :, None]).astype(jnp.bfloat16)
    state_mean = jnp.sum(tile_block, axis=1, dtype=jnp.float32) / members
    anomaly = (tile_block.astype(jnp.float32) - state_mean[:, None, :]).astype(jnp.bfloat16)
    update = jnp.einsum("tjk,tjc->tkc", weights, anomaly, preferred_element_type=jnp.float32)
    analysed = (state_mean[:, None, :] + update).astype(jnp.bfloat16)
    returned = lax.all_to_all(analysed[None], "mem", split_axis=2, concat_axis=0, tiled=True)
    returned = returned.reshape(strips, tile_count, block_members, 3, tile_columns, strip_rows)
    return jnp.transpose(returned, (2, 3, 1, 4, 0, 5)).reshape(block_members, 3, columns, latitudes)


def solution(mesh):
    in_specs = (
        P("mem", None, "band", None),
        P("band", None),
        P("mem", "band", None),
        P("mem", "band", None),
        P("mem", "band", None),
        P("mem", "band"),
    )
    out_specs = P("mem", None, "band", None)
    return jax.shard_map(
        on_device, mesh=mesh, in_specs=in_specs, out_specs=out_specs, check_vma=False
    )
```

profile of v0, /device:TPU:0, one launch (start us, length us, event | category | flops | bytes accessed | tf_op | source)
XLA Modules:
  0.0 279.9 jit_solution(7164611219929606275)
XLA Ops:
  0.0 2.0 fusion.1
  2.1 5.1 %collective-permute-start = (bf16[32,1,160]{2,0,1:T(8,128)(2,1)S(1)}, bf16[32,1,160]{2,0,1:T(8,128)(2,1)S(1)}, u32[]{:S(2)}, u32[]{:S(2)}) collective-permute-start(bf16[32,1,160]{2,0,1:T(8,128)(2,1)S(1)} %get-tuple-element.15), channel_id=1, source_target_pairs={{1,0},{2,1},{3,2},{0,3},{5,4},{6,5},{7,6},{4,7},{9,8},{10,9},{11,1... | collective-permute-start | bytes 30728 | tf_op jit(solution)/shard_map/ppermute | solution.py:22
  7.2 0.4 pad_convert_fusion
  7.6 1.0 collective-permute-done
  8.6 4.1 %collective-permute-done.1 = bf16[32,1,160]{2,0,1:T(8,128)(2,1)S(1)} collective-permute-done((bf16[32,1,160]{2,0,1:T(8,128)(2,1)S(1)}, bf16[32,1,160]{2,0,1:T(8,128)(2,1)S(1)}, u32[]{:S(2)}, u32[]{:S(2)}) %collective-permute-start.1) | collective-permute-done | bytes 10272 | tf_op jit(solution)/shard_map/ppermute | solution.py:20
  12.7 2.1 fusion.11
  14.9 3.8 %collective-permute-start.3 = (bf16[32,1,160]{2,0,1:T(8,128)(2,1)S(1)}, bf16[32,1,160]{2,0,1:T(8,128)(2,1)S(1)}, u32[]{:S(2)}, u32[]{:S(2)}) collective-permute-start(bf16[32,1,160]{2,0,1:T(8,128)(2,1)S(1)} %get-tuple-element.14), channel_id=1, source_target_pairs={{1,0},{2,1},{3,2},{0,3},{5,4},{6,5},{7,6},{4,7},{9,8},{10,9},{11,1... | collective-permute-start | bytes 30728 | tf_op jit(solution)/shard_map/ppermute | solution.py:22
  18.8 2.1 copy.30
  20.9 4.6 %stack.12 = bf16[32,1,2,30,8,20]{3,2,5,4,0,1:T(2,128)(2,1)S(1)} reshape(bf16[32,60,160]{1,2,0:T(8,128)(2,1)} %copy.30) | data formatting | bytes 1228800 | tf_op jit(solution)/shard_map/stack | solution.py:87
  25.4 1.5 maximum_convert_fusion
  26.9 0.2 slice.164
  27.1 1.6 copy-done.2
  28.7 2.6 fusion.3
  31.4 3.0 %copy.31 = bf16[32,60,160]{1,2,0:T(8,128)(2,1)} copy(bf16[32,60,160]{2,0,1:T(8,128)(2,1)} %get-tuple-element.9) | data formatting | bytes 1228800 | tf_op jit(solution)/shard_map/convert_element_type | solution.py:90
  34.4 5.6 %stack.13 = bf16[32,1,2,30,8,20]{3,2,5,4,0,1:T(2,128)(2,1)} reshape(bf16[32,60,160]{1,2,0:T(8,128)(2,1)} %copy.31) | data formatting | bytes 1228800 | tf_op jit(solution)/shard_map/stack | solution.py:87
  40.0 3.1 %copy.32 = bf16[32,60,160]{1,2,0:T(8,128)(2,1)} copy(bf16[32,60,160]{2,0,1:T(8,128)(2,1)} %get-tuple-element.10) | data formatting | bytes 1228800 | tf_op jit(solution)/shard_map/convert_element_type | solution.py:91
  43.1 5.6 %stack.14 = bf16[32,1,2,30,8,20]{3,2,5,4,0,1:T(2,128)(2,1)} reshape(bf16[32,60,160]{1,2,0:T(8,128)(2,1)} %copy.32) | data formatting | bytes 1228800 | tf_op jit(solution)/shard_map/stack | solution.py:87
  48.7 17.0 %maximum_bitcast_fusion = bf16[8,2,32,3,30,20]{4,1,5,0,2,3:T(2,128)(2,1)} fusion(bf16[32,1,2,30,8,20]{3,2,5,4,0,1:T(2,128)(2,1)} %stack.14, bf16[32,1,2,30,8,20]{3,2,5,4,0,1:T(2,128)(2,1)} %stack.13, bf16[32,1,2,30,8,20]{3,2,5,4,0,1:T(2,128)(2,1)S(1)} %stack.12), kind=kLoop, calls=%fused_computation.1 | loop fusion | flops 1843200 | bytes 3686400 | tf_op jit(solution)/shard_map/transpose | solution.py:98
  65.7 24.9 %copy.33 = bf16[8,2,32,3,30,20]{2,0,5,4,3,1:T(8,128)(2,1)} copy(bf16[8,2,32,3,30,20]{4,1,5,0,2,3:T(2,128)(2,1)} %maximum_bitcast_fusion) | data formatting | bytes 3686400 | tf_op jit(solution)/shard_map/transpose | solution.py:98
  90.6 9.1 %copy.34 = bf16[8,2,32,1800]{3,2,1,0:T(8,128)(2,1)} copy(bf16[8,2,32,1800]{2,0,3,1:T(8,128)(2,1)} %bitcast.114) | data formatting | bytes 3686400 | tf_op jit(solution)/shard_map/reshape | solution.py:98
  99.7 4.0 %all-to-all-start = ((bf16[8,2,32,1800]{3,2,1,0:T(8,128)(2,1)}), bf16[8,2,32,1800]{3,2,1,0:T(8,128)(2,1)S(1)}, u32[]{:S(2)}, u32[]{:S(2)}) async-start(bf16[8,2,32,1800]{3,2,1,0:T(8,128)(2,1)} %copy.34), calls=%async_computation | async-start | bytes 3932160 | tf_op jit(solution)/shard_map/all_to_all | solution.py:101
  103.8 25.0 %all-to-all-done = bf16[8,2,32,1800]{3,2,1,0:T(8,128)(2,1)S(1)} async-done(((bf16[8,2,32,1800]{3,2,1,0:T(8,128)(2,1)}), bf16[8,2,32,1800]{3,2,1,0:T(8,128)(2,1)S(1)}, u32[]{:S(2)}, u32[]{:S(2)}) %all-to-all-start) | async-done | bytes 1843232 | tf_op jit(solution)/shard_map/all_to_all | solution.py:101
  128.8 1.5 copy.35
  130.3 0.5 copy-done
  130.8 2.8 %copy.36 = bf16[2,256,1800]{1,2,0:T(8,128)(2,1)S(1)} copy(bf16[2,256,1800]{2,1,0:T(8,128)(2,1)} %bitcast.118) | data formatting | bytes 3686400 | tf_op jit(solution)/shard_map/squeeze | solution.py:101
  133.6 5.8 %gather_fusion = bf16[1024,256]{1,0:T(8,128)(2,1)S(1)} fusion(bf16[2,256,1800]{1,2,0:T(8,128)(2,1)S(1)} %copy.36, s32[1024]{0:T(1024)S(1)} %bitcast.113), kind=kCustom, calls=%fused_computation | custom fusion | bytes 1056768 | tf_op jit(solution)/shard_map/jit(take_along_axis)/gather | solution.py:103
  139.5 0.2 copy.37
  139.9 0.2 multiply_convert_fusion
  140.1 0.5 collective-permute-start.4
  140.8 2.3 collective-permute-start.9
  143.0 1.9 convert_reduce_fusion
  144.9 7.6 %collective-permute-done.5 = bf16[1,2,256,512]{3,2,1,0:T(8,128)(2,1)S(1)} collective-permute-done((bf16[1,2,256,512]{3,2,1,0:T(8,128)(2,1)S(1)}, bf16[1,2,256,512]{3,2,1,0:T(8,128)(2,1)S(1)}, u32[]{:S(2)}, u32[]{:S(2)}) %collective-permute-start.5) | collective-permute-done | bytes 524320 | tf_op jit(solution)/shard_map/ppermute | solution.py:22
  152.5 1.1 collective-permute-done.4
  153.5 0.2 pad_maximum_fusion.1
  153.7 0.2 fusion.60
  153.9 3.8 %collective-permute-start.7 = (bf16[3,1,256,512]{3,2,1,0:T(8,128)(2,1)S(1)}, bf16[3,1,256,512]{3,2,1,0:T(8,128)(2,1)S(1)}, u32[]{:S(2)}, u32[]{:S(2)}) collective-permute-start(bf16[3,1,256,512]{3,2,1,0:T(8,128)(2,1)S(1)} %get-tuple-element.12), channel_id=1, source_target_pairs={{1,0},{2,1},{3,2},{0,3},{5,4},{6,5},{7,6},{4,7},{9,8},{10,9},{11,1... | collective-permute-start | bytes 2359304 | tf_op jit(solution)/shard_map/ppermute | solution.py:22
  157.9 3.8 %collective-permute-start.11 = (bf16[3,1,512]{2,1,0:T(2,128)(2,1)S(1)}, bf16[3,1,512]{2,1,0:T(2,128)(2,1)S(1)}, u32[]{:S(2)}, u32[]{:S(2)}) collective-permute-start(bf16[3,1,512]{2,1,0:T(2,128)(2,1)S(1)} %get-tuple-element.18), channel_id=1, source_target_pairs={{1,0},{2,1},{3,2},{0,3},{5,4},{6,5},{7,6},{4,7},{9,8},{10,9},{11,1... | collective-permute-start | bytes 9224 | tf_op jit(solution)/shard_map/ppermute | solution.py:22
  161.7 29.6 %collective-permute-done.10 = bf16[3,1,512]{2,1,0:T(2,128)(2,1)S(1)} collective-permute-done((bf16[3,1,512]{2,1,0:T(2,128)(2,1)S(1)}, bf16[3,1,512]{2,1,0:T(2,128)(2,1)S(1)}, u32[]{:S(2)}, u32[]{:S(2)}) %collective-permute-start.10) | collective-permute-done | bytes 3104 | tf_op jit(solution)/shard_map/ppermute | solution.py:20
  191.4 1.3 fusion.58
  192.6 0.5 multiply_reduce_fusion
  193.1 0.7 fusion.17
  193.9 0.7 fusion.35
  194.5 0.6 fusion.29
  195.2 0.7 fusion.16
  195.9 0.7 fusion.65
  196.5 0.7 fusion.64
  197.2 0.7 fusion.15
  197.8 0.7 fusion.67
  198.5 0.7 fusion.66
  199.2 0.7 fusion.14
  199.8 0.7 fusion.68
  200.5 0.7 fusion.69
  201.2 1.3 fusion.36
  202.5 0.7 fusion.13
  203.2 0.7 fusion.70
  203.9 0.5 fusion.56
  204.4 0.6 fusion.54
  205.0 2.2 fusion
  207.2 5.1 %copy.39 = bf16[1,2,256,1800]{3,1,0,2:T(2,128)(2,1)S(1)} copy(bf16[1,2,256,1800]{2,3,1,0:T(8,128)(2,1)} %fusion) | data formatting | bytes 3686400 | tf_op jit(solution)/shard_map/broadcast_in_dim | solution.py:154
  212.3 28.6 %all_to_all.30 = bf16[1,2,256,1800]{3,1,0,2:T(2,128)(2,1)S(1)} all-to-all(bf16[1,2,256,1800]{3,1,0,2:T(2,128)(2,1)S(1)} %copy.39), channel_id=1, replica_groups=mesh['mem'=8,'band'=4] {'mem'}, dimensions={2} | all-to-all | bytes 3686400 | tf_op jit(solution)/shard_map/all_to_all | solution.py:154
  240.9 0.2 copy.40
  241.1 7.6 %copy.41 = bf16[8,1,2,32,1800]{3,0,4,2,1:T(8,128)(2,1)} copy(bf16[8,1,2,32,1800]{4,3,0,2,1:T(8,128)(2,1)S(1)} %bitcast.117) | data formatting | bytes 3686400 | tf_op jit(solution)/shard_map/all_to_all | solution.py:154
  248.6 16.8 %copy.50 = bf16[32,3,2,30,8,20]{5,4,0,3,2,1:T(8,128)(2,1)} copy(bf16[32,3,2,30,8,20]{0,4,5,3,1,2:T(8,128)(2,1)} %bitcast.115) | data formatting | bytes 3686400 | tf_op jit(solution)/shard_map/reshape | solution.py:156
  265.4 14.5 %reshape.287 = bf16[32,3,60,160]{3,0,2,1:T(8,128)(2,1)} reshape(bf16[32,3,2,30,8,20]{5,4,0,3,2,1:T(8,128)(2,1)} %copy.50) | data formatting | bytes 3686400 | tf_op jit(solution)/shard_map/reshape | solution.py:156
  (46 shorter events, 0.9 us)
Async XLA Ops:
  2.1 6.5 %collective-permute-start = (bf16[32,1,160]{2,0,1:T(8,128)(2,1)S(1)}, bf16[32,1,160]{2,0,1:T(8,128)(2,1)S(1)}, u32[]{:S(2)}, u32[]{:S(2)}) collective-permute-start(bf16[32,1,160]{2,0,1:T(8,128)(2,1)S(1)} %get-tuple-element.15), channel_id=1, source_target_pairs={{1,0},{2,1},{3,2},{0,3},{5,4},{6,5},{7,6},{4,7},{9,8},{10,9},{11,1... | collective-permute-start | bytes 30728 | tf_op jit(solution)/shard_map/ppermute | solution.py:22
  7.2 5.5 %collective-permute-start.1 = (bf16[32,1,160]{2,0,1:T(8,128)(2,1)S(1)}, bf16[32,1,160]{2,0,1:T(8,128)(2,1)S(1)}, u32[]{:S(2)}, u32[]{:S(2)}) collective-permute-start(bf16[32,1,160]{2,0,1:T(8,128)(2,1)S(1)} %get-tuple-element.16), channel_id=1, source_target_pairs={{0,1},{1,2},{2,3},{3,0},{4,5},{5,6},{6,7},{7,4},{8,9},{9,10},{10,1... | collective-permute-start | bytes 30728 | tf_op jit(solution)/shard_map/ppermute | solution.py:20
  14.8 4.0 %copy-start.1 = (bf16[32,60,160]{2,0,1:T(8,128)(2,1)}, bf16[32,60,160]{2,0,1:T(8,128)(2,1)S(1)}, u32[]{:S(2)}) copy-start(bf16[32,60,160]{2,0,1:T(8,128)(2,1)S(1)} %fusion.11) | copy-start | bytes 1843204
  14.8 10.6 %collective-permute-start.2 = (bf16[32,1,160]{2,0,1:T(8,128)(2,1)S(1)}, bf16[32,1,160]{2,0,1:T(8,128)(2,1)S(1)}, u32[]{:S(2)}, u32[]{:S(2)}) collective-permute-start(bf16[32,1,160]{2,0,1:T(8,128)(2,1)S(1)} %get-tuple-element.13), channel_id=1, source_target_pairs={{0,1},{1,2},{2,3},{3,0},{4,5},{5,6},{6,7},{7,4},{8,9},{9,10},{10,1... | collective-permute-start | bytes 30728 | tf_op jit(solution)/shard_map/ppermute | solution.py:20
  14.9 10.5 %collective-permute-start.3 = (bf16[32,1,160]{2,0,1:T(8,128)(2,1)S(1)}, bf16[32,1,160]{2,0,1:T(8,128)(2,1)S(1)}, u32[]{:S(2)}, u32[]{:S(2)}) collective-permute-start(bf16[32,1,160]{2,0,1:T(8,128)(2,1)S(1)} %get-tuple-element.14), channel_id=1, source_target_pairs={{1,0},{2,1},{3,2},{0,3},{5,4},{6,5},{7,6},{4,7},{9,8},{10,9},{11,1... | collective-permute-start | bytes 30728 | tf_op jit(solution)/shard_map/ppermute | solution.py:22
  26.9 1.8 copy-start.2
  99.7 4.0 %copy-start.3 = (s32[1,2,512]{2,1,0:T(2,128)S(1)}, s32[1,2,512]{2,1,0:T(2,128)}, u32[]{:S(2)}) copy-start(s32[1,2,512]{2,1,0:T(2,128)} %param.8) | copy-start | bytes 12292
  99.7 29.1 %all-to-all-start = ((bf16[8,2,32,1800]{3,2,1,0:T(8,128)(2,1)}), bf16[8,2,32,1800]{3,2,1,0:T(8,128)(2,1)S(1)}, u32[]{:S(2)}, u32[]{:S(2)}) async-start(bf16[8,2,32,1800]{3,2,1,0:T(8,128)(2,1)} %copy.34), calls=%async_computation | async-start | bytes 3932160 | tf_op jit(solution)/shard_map/all_to_all | solution.py:101
  128.8 2.0 copy-start
  133.6 6.2 %copy-start.4 = (f32[1,2,512]{2,1,0:T(2,128)S(1)}, f32[1,2,512]{2,1,0:T(2,128)}, u32[]{:S(2)}) copy-start(f32[1,2,512]{2,1,0:T(2,128)} %param.10) | copy-start | bytes 12292
  133.6 6.2 %copy-start.6 = (s32[1,2]{1,0:T(1,128)S(1)}, s32[1,2]{1,0:T(1,128)}, u32[]{:S(2)}) copy-start(s32[1,2]{1,0:T(1,128)} %param.11) | copy-start | bytes 28
  139.5 1.2 copy-start.5
  140.1 12.4 %collective-permute-start.5 = (bf16[1,2,256,512]{3,2,1,0:T(8,128)(2,1)S(1)}, bf16[1,2,256,512]{3,2,1,0:T(8,128)(2,1)S(1)}, u32[]{:S(2)}, u32[]{:S(2)}) collective-permute-start(bf16[1,2,256,512]{3,2,1,0:T(8,128)(2,1)S(1)} %multiply_convert_fusion), channel_id=1, source_target_pairs={{4,0},{8,4},{12,8},{16,12},{20,16},{24,20},{28,24},{0,28},{5,1},{9... | collective-permute-start | bytes 1572872 | tf_op jit(solution)/shard_map/ppermute | solution.py:22
  140.1 13.4 %collective-permute-start.4 = (bf16[1,2,256,512]{3,2,1,0:T(8,128)(2,1)S(1)}, bf16[1,2,256,512]{3,2,1,0:T(8,128)(2,1)S(1)}, u32[]{:S(2)}, u32[]{:S(2)}) collective-permute-start(bf16[1,2,256,512]{3,2,1,0:T(8,128)(2,1)S(1)} %multiply_convert_fusion), channel_id=1, source_target_pairs={{0,4},{4,8},{8,12},{12,16},{16,20},{20,24},{24,28},{28,0},{1,5},{5... | collective-permute-start | bytes 1572872 | tf_op jit(solution)/shard_map/ppermute | solution.py:20
  140.8 17.0 %collective-permute-start.9 = (bf16[1,2,512]{2,1,0:T(2,128)(2,1)S(1)}, bf16[1,2,512]{2,1,0:T(2,128)(2,1)S(1)}, u32[]{:S(2)}, u32[]{:S(2)}) collective-permute-start(bf16[1,2,512]{2,1,0:T(2,128)(2,1)S(1)} %fusion.45), channel_id=1, source_target_pairs={{4,0},{8,4},{12,8},{16,12},{20,16},{24,20},{28,24},{0,28},{5,1},{9... | collective-permute-start | bytes 6152 | tf_op jit(solution)/shard_map/ppermute | solution.py:22
  143.0 14.7 %collective-permute-start.8 = (bf16[1,2,512]{2,1,0:T(2,128)(2,1)S(1)}, bf16[1,2,512]{2,1,0:T(2,128)(2,1)S(1)}, u32[]{:S(2)}, u32[]{:S(2)}) collective-permute-start(bf16[1,2,512]{2,1,0:T(2,128)(2,1)S(1)} %fusion.45), channel_id=1, source_target_pairs={{0,4},{4,8},{8,12},{12,16},{16,20},{20,24},{24,28},{28,0},{1,5},{5... | collective-permute-start | bytes 6152 | tf_op jit(solution)/shard_map/ppermute | solution.py:20
  153.9 37.5 %collective-permute-start.6 = (bf16[3,1,256,512]{3,2,1,0:T(8,128)(2,1)S(1)}, bf16[3,1,256,512]{3,2,1,0:T(8,128)(2,1)S(1)}, u32[]{:S(2)}, u32[]{:S(2)}) collective-permute-start(bf16[3,1,256,512]{3,2,1,0:T(8,128)(2,1)S(1)} %get-tuple-element.11), channel_id=1, source_target_pairs={{0,1},{1,2},{2,3},{3,0},{4,5},{5,6},{6,7},{7,4},{8,9},{9,10},{10,1... | collective-permute-start | bytes 2359304 | tf_op jit(solution)/shard_map/ppermute | solution.py:20
  153.9 37.4 %collective-permute-start.7 = (bf16[3,1,256,512]{3,2,1,0:T(8,128)(2,1)S(1)}, bf16[3,1,256,512]{3,2,1,0:T(8,128)(2,1)S(1)}, u32[]{:S(2)}, u32[]{:S(2)}) collective-permute-start(bf16[3,1,256,512]{3,2,1,0:T(8,128)(2,1)S(1)} %get-tuple-element.12), channel_id=1, source_target_pairs={{1,0},{2,1},{3,2},{0,3},{5,4},{6,5},{7,6},{4,7},{9,8},{10,9},{11,1... | collective-permute-start | bytes 2359304 | tf_op jit(solution)/shard_map/ppermute | solution.py:22
  157.8 33.5 %collective-permute-start.10 = (bf16[3,1,512]{2,1,0:T(2,128)(2,1)S(1)}, bf16[3,1,512]{2,1,0:T(2,128)(2,1)S(1)}, u32[]{:S(2)}, u32[]{:S(2)}) collective-permute-start(bf16[3,1,512]{2,1,0:T(2,128)(2,1)S(1)} %get-tuple-element.17), channel_id=1, source_target_pairs={{0,1},{1,2},{2,3},{3,0},{4,5},{5,6},{6,7},{7,4},{8,9},{9,10},{10,1... | collective-permute-start | bytes 9224 | tf_op jit(solution)/shard_map/ppermute | solution.py:20
  157.9 33.4 %collective-permute-start.11 = (bf16[3,1,512]{2,1,0:T(2,128)(2,1)S(1)}, bf16[3,1,512]{2,1,0:T(2,128)(2,1)S(1)}, u32[]{:S(2)}, u32[]{:S(2)}) collective-permute-start(bf16[3,1,512]{2,1,0:T(2,128)(2,1)S(1)} %get-tuple-element.18), channel_id=1, source_target_pairs={{1,0},{2,1},{3,2},{0,3},{5,4},{6,5},{7,6},{4,7},{9,8},{10,9},{11,1... | collective-permute-start | bytes 9224 | tf_op jit(solution)/shard_map/ppermute | solution.py:22
where the time goes:
time: 282 us; the launch traced here: 280 us
  local copies, waits for them, and re-layouts  115 us (41%)
  waiting for transfers between devices  68.4 us (24%)
  other arithmetic  28.9 us (10%)
  blocking collectives  28.6 us (10%)
  starting transfers between devices  23.5 us (8%)
  matrix products  15.1 us (5%)
    ppermute x6, waiting for transfers between devices, padded_2(): lax.ppermute(tail, axis, [(i, (i + 1) % count) for i in range(count)])  34.8 us
    reshape x2, local copies, waits for them, and re-layouts, on_device(): jnp.transpose(returned, (2, 3, 1, 4, 0, 5))  31.3 us
    all_to_all x1, blocking collectives, on_device(): lax.all_to_all(analysed[None], 'mem', split_axis=2, concat_axis=0, tiled=...  28.6 us
    all_to_all x1, waiting for transfers between devices, on_device(): lax.all_to_all(reordered, 'mem', split_axis=0, concat_axis=2, tiled=True)[0]  25 us
    transpose x1, local copies, waits for them, and re-layouts, on_device(): jnp.transpose(reordered, (4, 2, 0, 1, 3, 5))  24.9 us
    ppermute x6, starting transfers between devices, padded_2(): lax.ppermute(head, axis, [((i + 1) % count, i) for i in range(count)])  18.8 us
    transpose x1, other arithmetic, on_device(): jnp.transpose(reordered, (4, 2, 0, 1, 3, 5))  17 us
    another operation x3, local copies, waits for them, and re-layouts, on_device(): jnp.stack([surface_elevation_cast, revised_zonal_velocity.astype(jnp.bflo...  15.8 us
  transfers between devices with their start and end apart: 13, of which 6 were waited for; matrix products, arithmetic and copies ran while one was open for 3% of the time, Pallas kernels for 0%

commit v1 on v0

--- a/solution.py
+++ b/solution.py
@@ -8,6 +8,29 @@
 half_step = 0.1
 coriolis_scale = 0.3
 neighbour_weight = 0.75
+
+
+def split_up(x, dim, length):
+    dims = x.shape
+    tiles = x.reshape(*dims[:dim], length, dims[dim] // length, *dims[dim + 1 :])
+    return jnp.moveaxis(tiles, dim, 0)
+
+
+def laid_out(tiles, dim):
+    shape = list(tiles.shape[1:])
+    shape[dim] *= tiles.shape[0]
+    return jnp.moveaxis(tiles, 0, dim).reshape(shape)
+
+
+def exchange_in_pairs(x, axis, split_dim, concat_dim):
+    peers, index = (lax.axis_size(axis), lax.axis_index(axis))
+    parts = split_up(x, split_dim, peers)
+    done = [parts[index]]
+    for lap in range(1, peers):
+        sent = parts[index ^ lap]
+        done.append(lax.ppermute(sent, axis, [(i, i ^ lap) for i in range(peers)]))
+    parts = jnp.stack(done)[index ^ jnp.arange(peers)]
+    return laid_out(parts, concat_dim)
 
 
 def padded_2(cells, sides, width):
@@ -151,7 +174,7 @@
     anomaly = (tile_block.astype(jnp.float32) - state_mean[:, None, :]).astype(jnp.bfloat16)
     update = jnp.einsum("tjk,tjc->tkc", weights, anomaly, preferred_element_type=jnp.float32)
     analysed = (state_mean[:, None, :] + update).astype(jnp.bfloat16)
-    returned = lax.all_to_all(analysed[None], "mem", split_axis=2, concat_axis=0, tiled=True)
+    returned = exchange_in_pairs(analysed[None], "mem", 2, 0)
     returned = returned.reshape(strips, tile_count, block_members, 3, tile_columns, strip_rows)
     return jnp.transpose(returned, (2, 3, 1, 4, 0, 5)).reshape(block_members, 3, columns, latitudes)
 

time: 282 us -> 281 us (level)
  blocking collectives: 28.6 us -> 0 us
  waiting for transfers between devices: 68.4 us -> 85.1 us
  starting transfers between devices: 23.5 us -> 31.8 us
    all_to_all x1 -> x0, blocking collectives: 28.6 us -> none  [on_device(): lax.all_to_all(analysed[None], 'mem', split_axis=2, concat_axis=0, tiled=...]
    ppermute x0 -> x7, waiting for transfers between devices: none -> 17.5 us  [exchange_in_pairs(): done.append(lax.ppermute(sent, axis, [(i, i ^ lap) for i in range(peers)]))]
    gather x0 -> x2, local copies, waits for them, and re-layouts: none -> 9.93 us  [exchange_in_pairs(): parts = jnp.stack(done)[index ^ jnp.arange(peers)]]
    ppermute x0 -> x7, starting transfers between devices: none -> 8.31 us  [exchange_in_pairs(): done.append(lax.ppermute(sent, axis, [(i, i ^ lap) for i in range(peers)]))]
    all_to_all x2 -> x0, local copies, waits for them, and re-layouts: 7.75 us -> none  [on_device(): lax.all_to_all(analysed[None], 'mem', split_axis=2, concat_axis=0, tiled=...]
    broadcast_in_dim x1 -> x0, local copies, waits for them, and re-layouts: 5.08 us -> none  [on_device(): analysed[None]]
  transfers between devices with their start and end apart: 13 -> 20, of which waited for: 6 -> 9; matrix products, arithmetic and copies ran while one was open for 3% -> 4% of each run, Pallas kernels for 0% -> 0%
where the time goes in v1:
time: 281 us; the launch traced here: 279 us
  local copies, waits for them, and re-layouts  116 us (41%)
  waiting for transfers between devices  85.1 us (30%)
  starting transfers between devices  31.8 us (11%)
  other arithmetic  29.7 us (11%)
  matrix products  15.1 us (5%)
    ppermute x6, waiting for transfers between devices, padded_2(): lax.ppermute(tail, axis, [(i, (i + 1) % count) for i in range(count)])  34.8 us
    reshape x2, local copies, waits for them, and re-layouts, on_device(): jnp.transpose(returned, (2, 3, 1, 4, 0, 5))  31.3 us
    transpose x1, local copies, waits for them, and re-layouts, on_device(): jnp.transpose(reordered, (4, 2, 0, 1, 3, 5))  24.9 us
    all_to_all x1, waiting for transfers between devices, on_device(): lax.all_to_all(reordered, 'mem', split_axis=0, concat_axis=2, tiled=True)[0]  24.2 us
    ppermute x6, starting transfers between devices, padded_2(): lax.ppermute(head, axis, [((i + 1) % count, i) for i in range(count)])  18.8 us
    ppermute x7, waiting for transfers between devices, exchange_in_pairs(): done.append(lax.ppermute(sent, axis, [(i, i ^ lap) for i in range(peers)]))  17.5 us
    transpose x1, other arithmetic, on_device(): jnp.transpose(reordered, (4, 2, 0, 1, 3, 5))  17.1 us
    another operation x3, local copies, waits for them, and re-layouts, on_device(): jnp.stack([surface_elevation_cast, revised_zonal_velocity.astype(jnp.bflo...  15.8 us
  transfers between devices with their start and end apart: 20, of which 9 were waited for; matrix products, arithmetic and copies ran while one was open for 4% of the time, Pallas kernels for 0%

profile of v1, /device:TPU:0, one launch (start us, length us, event | category | flops | bytes accessed | tf_op | source)
XLA Modules:
  0.0 278.8 jit_solution(3285994092311827240)
XLA Ops:
  0.0 2.0 fusion
  2.1 5.1 %collective-permute-start = (bf16[32,1,160]{2,0,1:T(8,128)(2,1)S(1)}, bf16[32,1,160]{2,0,1:T(8,128)(2,1)S(1)}, u32[]{:S(2)}, u32[]{:S(2)}) collective-permute-start(bf16[32,1,160]{2,0,1:T(8,128)(2,1)S(1)} %get-tuple-element.22), channel_id=1, source_target_pairs={{1,0},{2,1},{3,2},{0,3},{5,4},{6,5},{7,6},{4,7},{9,8},{10,9},{11,1... | collective-permute-start | bytes 30728 | tf_op jit(solution)/shard_map/ppermute | solution.py:45
  7.6 1.0 collective-permute-done
  8.6 4.1 %collective-permute-done.1 = bf16[32,1,160]{2,0,1:T(8,128)(2,1)S(1)} collective-permute-done((bf16[32,1,160]{2,0,1:T(8,128)(2,1)S(1)}, bf16[32,1,160]{2,0,1:T(8,128)(2,1)S(1)}, u32[]{:S(2)}, u32[]{:S(2)}) %collective-permute-start.1) | collective-permute-done | bytes 10272 | tf_op jit(solution)/shard_map/ppermute | solution.py:43
  12.7 2.1 fusion.10
  14.9 3.8 %collective-permute-start.3 = (bf16[32,1,160]{2,0,1:T(8,128)(2,1)S(1)}, bf16[32,1,160]{2,0,1:T(8,128)(2,1)S(1)}, u32[]{:S(2)}, u32[]{:S(2)}) collective-permute-start(bf16[32,1,160]{2,0,1:T(8,128)(2,1)S(1)} %get-tuple-element.21), channel_id=1, source_target_pairs={{1,0},{2,1},{3,2},{0,3},{5,4},{6,5},{7,6},{4,7},{9,8},{10,9},{11,1... | collective-permute-start | bytes 30728 | tf_op jit(solution)/shard_map/ppermute | solution.py:45
  18.8 2.1 copy.30
  20.9 4.6 %stack.36 = bf16[32,1,2,30,8,20]{3,2,5,4,0,1:T(2,128)(2,1)S(1)} reshape(bf16[32,60,160]{1,2,0:T(8,128)(2,1)} %copy.30) | data formatting | bytes 1228800 | tf_op jit(solution)/shard_map/stack | solution.py:110
  25.4 1.5 maximum_convert_fusion
  27.1 1.6 copy-done.2
  28.7 2.7 fusion.2
  31.4 3.0 %copy.31 = bf16[32,60,160]{1,2,0:T(8,128)(2,1)} copy(bf16[32,60,160]{2,0,1:T(8,128)(2,1)} %get-tuple-element.9) | data formatting | bytes 1228800 | tf_op jit(solution)/shard_map/convert_element_type | solution.py:113
  34.4 5.6 %stack.37 = bf16[32,1,2,30,8,20]{3,2,5,4,0,1:T(2,128)(2,1)} reshape(bf16[32,60,160]{1,2,0:T(8,128)(2,1)} %copy.31) | data formatting | bytes 1228800 | tf_op jit(solution)/shard_map/stack | solution.py:110
  40.1 3.1 %copy.32 = bf16[32,60,160]{1,2,0:T(8,128)(2,1)} copy(bf16[32,60,160]{2,0,1:T(8,128)(2,1)} %get-tuple-element.10) | data formatting | bytes 1228800 | tf_op jit(solution)/shard_map/convert_element_type | solution.py:114
  43.2 5.6 %stack.38 = bf16[32,1,2,30,8,20]{3,2,5,4,0,1:T(2,128)(2,1)} reshape(bf16[32,60,160]{1,2,0:T(8,128)(2,1)} %copy.32) | data formatting | bytes 1228800 | tf_op jit(solution)/shard_map/stack | solution.py:110
  48.8 17.1 %maximum_bitcast_fusion = bf16[8,2,32,3,30,20]{4,1,5,0,2,3:T(2,128)(2,1)} fusion(bf16[32,1,2,30,8,20]{3,2,5,4,0,1:T(2,128)(2,1)} %stack.38, bf16[32,1,2,30,8,20]{3,2,5,4,0,1:T(2,128)(2,1)} %stack.37, bf16[32,1,2,30,8,20]{3,2,5,4,0,1:T(2,128)(2,1)S(1)} %stack.36), kind=kLoop, calls=%fused_computation.2 | loop fusion | flops 1843200 | bytes 3686400 | tf_op jit(solution)/shard_map/transpose | solution.py:121
  65.9 24.9 %copy.33 = bf16[8,2,32,3,30,20]{2,0,5,4,3,1:T(8,128)(2,1)} copy(bf16[8,2,32,3,30,20]{4,1,5,0,2,3:T(2,128)(2,1)} %maximum_bitcast_fusion) | data formatting | bytes 3686400 | tf_op jit(solution)/shard_map/transpose | solution.py:121
  90.8 9.1 %copy.34 = bf16[8,2,32,1800]{3,2,1,0:T(8,128)(2,1)} copy(bf16[8,2,32,1800]{2,0,3,1:T(8,128)(2,1)} %bitcast.143) | data formatting | bytes 3686400 | tf_op jit(solution)/shard_map/reshape | solution.py:121
  99.8 4.0 %all-to-all-start = ((bf16[8,2,32,1800]{3,2,1,0:T(8,128)(2,1)}), bf16[8,2,32,1800]{3,2,1,0:T(8,128)(2,1)S(1)}, u32[]{:S(2)}, u32[]{:S(2)}) async-start(bf16[8,2,32,1800]{3,2,1,0:T(8,128)(2,1)} %copy.34), calls=%async_computation | async-start | bytes 3932160 | tf_op jit(solution)/shard_map/all_to_all | solution.py:124
  104.0 0.7 fusion.31
  104.7 24.2 %all-to-all-done = bf16[8,2,32,1800]{3,2,1,0:T(8,128)(2,1)S(1)} async-done(((bf16[8,2,32,1800]{3,2,1,0:T(8,128)(2,1)}), bf16[8,2,32,1800]{3,2,1,0:T(8,128)(2,1)S(1)}, u32[]{:S(2)}, u32[]{:S(2)}) %all-to-all-start) | async-done | bytes 1843232 | tf_op jit(solution)/shard_map/all_to_all | solution.py:124
  128.9 1.5 copy.35
  130.9 2.8 %copy.36 = bf16[2,256,1800]{1,2,0:T(8,128)(2,1)S(1)} copy(bf16[2,256,1800]{2,1,0:T(8,128)(2,1)} %bitcast.148) | data formatting | bytes 3686400 | tf_op jit(solution)/shard_map/squeeze | solution.py:124
  133.8 5.8 %gather_fusion.1 = bf16[1024,256]{1,0:T(8,128)(2,1)S(1)} fusion(bf16[2,256,1800]{1,2,0:T(8,128)(2,1)S(1)} %copy.36, s32[1024]{0:T(1024)S(1)} %bitcast.142), kind=kCustom, calls=%fused_computation.1 | custom fusion | bytes 1056768 | tf_op jit(solution)/shard_map/jit(take_along_axis)/gather | solution.py:126
  140.9 2.3 collective-permute-start.9
  143.1 1.9 convert_reduce_fusion
  145.0 7.6 %collective-permute-done.5 = bf16[1,2,256,512]{3,2,1,0:T(8,128)(2,1)S(1)} collective-permute-done((bf16[1,2,256,512]{3,2,1,0:T(8,128)(2,1)S(1)}, bf16[1,2,256,512]{3,2,1,0:T(8,128)(2,1)S(1)}, u32[]{:S(2)}, u32[]{:S(2)}) %collective-permute-start.5) | collective-permute-done | bytes 524320 | tf_op jit(solution)/shard_map/ppermute | solution.py:45
  152.6 1.1 collective-permute-done.4
  154.1 3.8 %collective-permute-start.7 = (bf16[3,1,256,512]{3,2,1,0:T(8,128)(2,1)S(1)}, bf16[3,1,256,512]{3,2,1,0:T(8,128)(2,1)S(1)}, u32[]{:S(2)}, u32[]{:S(2)}) collective-permute-start(bf16[3,1,256,512]{3,2,1,0:T(8,128)(2,1)S(1)} %get-tuple-element.19), channel_id=1, source_target_pairs={{1,0},{2,1},{3,2},{0,3},{5,4},{6,5},{7,6},{4,7},{9,8},{10,9},{11,1... | collective-permute-start | bytes 2359304 | tf_op jit(solution)/shard_map/ppermute | solution.py:45
  158.0 3.8 %collective-permute-start.11 = (bf16[3,1,512]{2,1,0:T(2,128)(2,1)S(1)}, bf16[3,1,512]{2,1,0:T(2,128)(2,1)S(1)}, u32[]{:S(2)}, u32[]{:S(2)}) collective-permute-start(bf16[3,1,512]{2,1,0:T(2,128)(2,1)S(1)} %get-tuple-element.25), channel_id=1, source_target_pairs={{1,0},{2,1},{3,2},{0,3},{5,4},{6,5},{7,6},{4,7},{9,8},{10,9},{11,1... | collective-permute-start | bytes 9224 | tf_op jit(solution)/shard_map/ppermute | solution.py:45
  161.8 29.6 %collective-permute-done.10 = bf16[3,1,512]{2,1,0:T(2,128)(2,1)S(1)} collective-permute-done((bf16[3,1,512]{2,1,0:T(2,128)(2,1)S(1)}, bf16[3,1,512]{2,1,0:T(2,128)(2,1)S(1)}, u32[]{:S(2)}, u32[]{:S(2)}) %collective-permute-start.10) | collective-permute-done | bytes 3104 | tf_op jit(solution)/shard_map/ppermute | solution.py:43
  191.5 1.3 fusion.58
  193.3 0.7 fusion.16
  194.0 0.7 fusion.34
  194.7 0.6 fusion.28
  195.3 0.7 fusion.15
  196.0 0.7 fusion.65
  196.7 0.7 fusion.64
  197.3 0.7 fusion.14
  198.0 0.7 fusion.67
  198.7 0.7 fusion.66
  199.3 0.7 fusion.13
  200.0 0.7 fusion.68
  200.6 0.7 fusion.69
  201.3 1.3 fusion.35
  202.7 0.7 fusion.12
  203.4 0.7 fusion.70
  204.0 0.5 fusion.55
  204.6 0.6 fusion.53
  205.2 2.2 add_convert_fusion
  207.4 2.8 copy.39
  210.3 1.9 collective-permute-start.18
  212.2 1.6 collective-permute-start.16
  213.8 0.9 collective-permute-start.15
  214.8 1.5 collective-permute-done.12
  216.3 2.3 collective-permute-start.13
  218.6 9.9 %collective-permute-done.13 = bf16[1,2,32,1800]{3,2,1,0:T(8,128)(2,1)S(1)} collective-permute-done((bf16[1,2,32,1800]{3,2,1,0:T(8,128)(2,1)S(1)}, bf16[1,2,32,1800]{3,2,1,0:T(8,128)(2,1)S(1)}, u32[]{:S(2)}, u32[]{:S(2)}) %collective-permute-start.13) | collective-permute-done | bytes 230432 | tf_op jit(solution)/shard_map/ppermute | solution.py:31
  228.5 1.6 collective-permute-start.14
  230.1 6.1 %collective-permute-done.14 = bf16[1,2,32,1800]{3,2,1,0:T(8,128)(2,1)S(1)} collective-permute-done((bf16[1,2,32,1800]{3,2,1,0:T(8,128)(2,1)S(1)}, bf16[1,2,32,1800]{3,2,1,0:T(8,128)(2,1)S(1)}, u32[]{:S(2)}, u32[]{:S(2)}) %collective-permute-start.14) | collective-permute-done | bytes 230432 | tf_op jit(solution)/shard_map/ppermute | solution.py:31
  236.3 1.3 copy-done.3
  237.6 2.4 gather_fusion
  240.0 7.6 %copy.40 = bf16[8,2,32,1800]{2,0,3,1:T(8,128)(2,1)} copy(bf16[8,2,32,1800]{3,2,1,0:T(8,128)(2,1)S(1)} %gather_fusion) | data formatting | bytes 3686400 | tf_op jit(solution)/shard_map/gather | solution.py:32
  247.5 16.8 %copy.49 = bf16[32,3,2,30,8,20]{5,4,0,3,2,1:T(8,128)(2,1)} copy(bf16[32,3,2,30,8,20]{0,4,5,3,1,2:T(8,128)(2,1)} %bitcast.144) | data formatting | bytes 3686400 | tf_op jit(solution)/shard_map/reshape | solution.py:179
  264.3 14.5 %reshape.324 = bf16[32,3,60,160]{3,0,2,1:T(8,128)(2,1)} reshape(bf16[32,3,2,30,8,20]{5,4,0,3,2,1:T(8,128)(2,1)} %copy.49) | data formatting | bytes 3686400 | tf_op jit(solution)/shard_map/reshape | solution.py:179
  (74 shorter events, 4.0 us)
Async XLA Ops:
  2.1 6.5 %collective-permute-start = (bf16[32,1,160]{2,0,1:T(8,128)(2,1)S(1)}, bf16[32,1,160]{2,0,1:T(8,128)(2,1)S(1)}, u32[]{:S(2)}, u32[]{:S(2)}) collective-permute-start(bf16[32,1,160]{2,0,1:T(8,128)(2,1)S(1)} %get-tuple-element.22), channel_id=1, source_target_pairs={{1,0},{2,1},{3,2},{0,3},{5,4},{6,5},{7,6},{4,7},{9,8},{10,9},{11,1... | collective-permute-start | bytes 30728 | tf_op jit(solution)/shard_map/ppermute | solution.py:45
  7.2 5.5 %collective-permute-start.1 = (bf16[32,1,160]{2,0,1:T(8,128)(2,1)S(1)}, bf16[32,1,160]{2,0,1:T(8,128)(2,1)S(1)}, u32[]{:S(2)}, u32[]{:S(2)}) collective-permute-start(bf16[32,1,160]{2,0,1:T(8,128)(2,1)S(1)} %get-tuple-element.23), channel_id=1, source_target_pairs={{0,1},{1,2},{2,3},{3,0},{4,5},{5,6},{6,7},{7,4},{8,9},{9,10},{10,1... | collective-permute-start | bytes 30728 | tf_op jit(solution)/shard_map/ppermute | solution.py:43
  14.8 4.0 %copy-start.1 = (bf16[32,60,160]{2,0,1:T(8,128)(2,1)}, bf16[32,60,160]{2,0,1:T(8,128)(2,1)S(1)}, u32[]{:S(2)}) copy-start(bf16[32,60,160]{2,0,1:T(8,128)(2,1)S(1)} %fusion.10) | copy-start | bytes 1843204
  14.8 10.6 %collective-permute-start.2 = (bf16[32,1,160]{2,0,1:T(8,128)(2,1)S(1)}, bf16[32,1,160]{2,0,1:T(8,128)(2,1)S(1)}, u32[]{:S(2)}, u32[]{:S(2)}) collective-permute-start(bf16[32,1,160]{2,0,1:T(8,128)(2,1)S(1)} %get-tuple-element.20), channel_id=1, source_target_pairs={{0,1},{1,2},{2,3},{3,0},{4,5},{5,6},{6,7},{7,4},{8,9},{9,10},{10,1... | collective-permute-start | bytes 30728 | tf_op jit(solution)/shard_map/ppermute | solution.py:43
  14.9 10.5 %collective-permute-start.3 = (bf16[32,1,160]{2,0,1:T(8,128)(2,1)S(1)}, bf16[32,1,160]{2,0,1:T(8,128)(2,1)S(1)}, u32[]{:S(2)}, u32[]{:S(2)}) collective-permute-start(bf16[32,1,160]{2,0,1:T(8,128)(2,1)S(1)} %get-tuple-element.21), channel_id=1, source_target_pairs={{1,0},{2,1},{3,2},{0,3},{5,4},{6,5},{7,6},{4,7},{9,8},{10,9},{11,1... | collective-permute-start | bytes 30728 | tf_op jit(solution)/shard_map/ppermute | solution.py:45
  26.9 1.8 copy-start.2
  99.8 4.0 %copy-start.5 = (s32[1,2,512]{2,1,0:T(2,128)S(1)}, s32[1,2,512]{2,1,0:T(2,128)}, u32[]{:S(2)}) copy-start(s32[1,2,512]{2,1,0:T(2,128)} %param.8) | copy-start | bytes 12292
  99.8 29.1 %all-to-all-start = ((bf16[8,2,32,1800]{3,2,1,0:T(8,128)(2,1)}), bf16[8,2,32,1800]{3,2,1,0:T(8,128)(2,1)S(1)}, u32[]{:S(2)}, u32[]{:S(2)}) async-start(bf16[8,2,32,1800]{3,2,1,0:T(8,128)(2,1)} %copy.34), calls=%async_computation | async-start | bytes 3932160 | tf_op jit(solution)/shard_map/all_to_all | solution.py:124
  128.9 2.0 copy-start
  133.7 6.2 %copy-start.6 = (f32[1,2,512]{2,1,0:T(2,128)S(1)}, f32[1,2,512]{2,1,0:T(2,128)}, u32[]{:S(2)}) copy-start(f32[1,2,512]{2,1,0:T(2,128)} %param.10) | copy-start | bytes 12292
  133.8 6.2 %copy-start.8 = (s32[1,2]{1,0:T(1,128)S(1)}, s32[1,2]{1,0:T(1,128)}, u32[]{:S(2)}) copy-start(s32[1,2]{1,0:T(1,128)} %param.11) | copy-start | bytes 28
  139.6 1.2 copy-start.7
  140.2 12.4 %collective-permute-start.5 = (bf16[1,2,256,512]{3,2,1,0:T(8,128)(2,1)S(1)}, bf16[1,2,256,512]{3,2,1,0:T(8,128)(2,1)S(1)}, u32[]{:S(2)}, u32[]{:S(2)}) collective-permute-start(bf16[1,2,256,512]{3,2,1,0:T(8,128)(2,1)S(1)} %multiply_convert_fusion), channel_id=1, source_target_pairs={{4,0},{8,4},{12,8},{16,12},{20,16},{24,20},{28,24},{0,28},{5,1},{9... | collective-permute-start | bytes 1572872 | tf_op jit(solution)/shard_map/ppermute | solution.py:45
  140.3 13.4 %collective-permute-start.4 = (bf16[1,2,256,512]{3,2,1,0:T(8,128)(2,1)S(1)}, bf16[1,2,256,512]{3,2,1,0:T(8,128)(2,1)S(1)}, u32[]{:S(2)}, u32[]{:S(2)}) collective-permute-start(bf16[1,2,256,512]{3,2,1,0:T(8,128)(2,1)S(1)} %multiply_convert_fusion), channel_id=1, source_target_pairs={{0,4},{4,8},{8,12},{12,16},{16,20},{20,24},{24,28},{28,0},{1,5},{5... | collective-permute-start | bytes 1572872 | tf_op jit(solution)/shard_map/ppermute | solution.py:43
  140.9 17.0 %collective-permute-start.9 = (bf16[1,2,512]{2,1,0:T(2,128)(2,1)S(1)}, bf16[1,2,512]{2,1,0:T(2,128)(2,1)S(1)}, u32[]{:S(2)}, u32[]{:S(2)}) collective-permute-start(bf16[1,2,512]{2,1,0:T(2,128)(2,1)S(1)} %fusion.44), channel_id=1, source_target_pairs={{4,0},{8,4},{12,8},{16,12},{20,16},{24,20},{28,24},{0,28},{5,1},{9... | collective-permute-start | bytes 6152 | tf_op jit(solution)/shard_map/ppermute | solution.py:45
  143.1 14.8 %collective-permute-start.8 = (bf16[1,2,512]{2,1,0:T(2,128)(2,1)S(1)}, bf16[1,2,512]{2,1,0:T(2,128)(2,1)S(1)}, u32[]{:S(2)}, u32[]{:S(2)}) collective-permute-start(bf16[1,2,512]{2,1,0:T(2,128)(2,1)S(1)} %fusion.44), channel_id=1, source_target_pairs={{0,4},{4,8},{8,12},{12,16},{16,20},{20,24},{24,28},{28,0},{1,5},{5... | collective-permute-start | bytes 6152 | tf_op jit(solution)/shard_map/ppermute | solution.py:43
  154.0 37.5 %collective-permute-start.6 = (bf16[3,1,256,512]{3,2,1,0:T(8,128)(2,1)S(1)}, bf16[3,1,256,512]{3,2,1,0:T(8,128)(2,1)S(1)}, u32[]{:S(2)}, u32[]{:S(2)}) collective-permute-start(bf16[3,1,256,512]{3,2,1,0:T(8,128)(2,1)S(1)} %get-tuple-element.18), channel_id=1, source_target_pairs={{0,1},{1,2},{2,3},{3,0},{4,5},{5,6},{6,7},{7,4},{8,9},{9,10},{10,1... | collective-permute-start | bytes 2359304 | tf_op jit(solution)/shard_map/ppermute | solution.py:43
  154.1 37.4 %collective-permute-start.7 = (bf16[3,1,256,512]{3,2,1,0:T(8,128)(2,1)S(1)}, bf16[3,1,256,512]{3,2,1,0:T(8,128)(2,1)S(1)}, u32[]{:S(2)}, u32[]{:S(2)}) collective-permute-start(bf16[3,1,256,512]{3,2,1,0:T(8,128)(2,1)S(1)} %get-tuple-element.19), channel_id=1, source_target_pairs={{1,0},{2,1},{3,2},{0,3},{5,4},{6,5},{7,6},{4,7},{9,8},{10,9},{11,1... | collective-permute-start | bytes 2359304 | tf_op jit(solution)/shard_map/ppermute | solution.py:45
  157.9 33.5 %collective-permute-start.10 = (bf16[3,1,512]{2,1,0:T(2,128)(2,1)S(1)}, bf16[3,1,512]{2,1,0:T(2,128)(2,1)S(1)}, u32[]{:S(2)}, u32[]{:S(2)}) collective-permute-start(bf16[3,1,512]{2,1,0:T(2,128)(2,1)S(1)} %get-tuple-element.24), channel_id=1, source_target_pairs={{0,1},{1,2},{2,3},{3,0},{4,5},{5,6},{6,7},{7,4},{8,9},{9,10},{10,1... | collective-permute-start | bytes 9224 | tf_op jit(solution)/shard_map/ppermute | solution.py:43
  158.0 33.4 %collective-permute-start.11 = (bf16[3,1,512]{2,1,0:T(2,128)(2,1)S(1)}, bf16[3,1,512]{2,1,0:T(2,128)(2,1)S(1)}, u32[]{:S(2)}, u32[]{:S(2)}) collective-permute-start(bf16[3,1,512]{2,1,0:T(2,128)(2,1)S(1)} %get-tuple-element.25), channel_id=1, source_target_pairs={{1,0},{2,1},{3,2},{0,3},{5,4},{6,5},{7,6},{4,7},{9,8},{10,9},{11,1... | collective-permute-start | bytes 9224 | tf_op jit(solution)/shard_map/ppermute | solution.py:45
  191.5 1.3 copy-start.4
  210.3 26.0 %collective-permute-start.18 = (bf16[1,2,32,1800]{3,2,1,0:T(8,128)(2,1)S(1)}, bf16[1,2,32,1800]{3,2,1,0:T(8,128)(2,1)S(1)}, u32[]{:S(2)}, u32[]{:S(2)}) collective-permute-start(bf16[1,2,32,1800]{3,2,1,0:T(8,128)(2,1)S(1)} %get-tuple-element.11), channel_id=1, source_target_pairs={{0,28},{4,24},{8,20},{12,16},{16,12},{20,8},{24,4},{28,0},{1,29},{... | collective-permute-start | bytes 691208 | tf_op jit(solution)/shard_map/ppermute | solution.py:31
  212.2 24.0 %collective-permute-start.17 = (bf16[1,2,32,1800]{3,2,1,0:T(8,128)(2,1)S(1)}, bf16[1,2,32,1800]{3,2,1,0:T(8,128)(2,1)S(1)}, u32[]{:S(2)}, u32[]{:S(2)}) collective-permute-start(bf16[1,2,32,1800]{3,2,1,0:T(8,128)(2,1)S(1)} %get-tuple-element.12), channel_id=1, source_target_pairs={{0,24},{4,28},{8,16},{12,20},{16,8},{20,12},{24,0},{28,4},{1,25},{... | collective-permute-start | bytes 691208 | tf_op jit(solution)/shard_map/ppermute | solution.py:31
  212.2 23.9 %collective-permute-start.16 = (bf16[1,2,32,1800]{3,2,1,0:T(8,128)(2,1)S(1)}, bf16[1,2,32,1800]{3,2,1,0:T(8,128)(2,1)S(1)}, u32[]{:S(2)}, u32[]{:S(2)}) collective-permute-start(bf16[1,2,32,1800]{3,2,1,0:T(8,128)(2,1)S(1)} %get-tuple-element.13), channel_id=1, source_target_pairs={{0,20},{4,16},{8,28},{12,24},{16,4},{20,0},{24,12},{28,8},{1,21},{... | collective-permute-start | bytes 691208 | tf_op jit(solution)/shard_map/ppermute | solution.py:31
  213.8 22.3 %collective-permute-start.15 = (bf16[1,2,32,1800]{3,2,1,0:T(8,128)(2,1)S(1)}, bf16[1,2,32,1800]{3,2,1,0:T(8,128)(2,1)S(1)}, u32[]{:S(2)}, u32[]{:S(2)}) collective-permute-start(bf16[1,2,32,1800]{3,2,1,0:T(8,128)(2,1)S(1)} %get-tuple-element.14), channel_id=1, source_target_pairs={{0,16},{4,20},{8,24},{12,28},{16,0},{20,4},{24,8},{28,12},{1,17},{... | collective-permute-start | bytes 691208 | tf_op jit(solution)/shard_map/ppermute | solution.py:31
  214.8 1.5 collective-permute-start.12
  216.3 12.2 %collective-permute-start.13 = (bf16[1,2,32,1800]{3,2,1,0:T(8,128)(2,1)S(1)}, bf16[1,2,32,1800]{3,2,1,0:T(8,128)(2,1)S(1)}, u32[]{:S(2)}, u32[]{:S(2)}) collective-permute-start(bf16[1,2,32,1800]{3,2,1,0:T(8,128)(2,1)S(1)} %get-tuple-element.16), channel_id=1, source_target_pairs={{0,8},{4,12},{8,0},{12,4},{16,24},{20,28},{24,16},{28,20},{1,9},{5... | collective-permute-start | bytes 691208 | tf_op jit(solution)/shard_map/ppermute | solution.py:31
  228.5 7.6 %collective-permute-start.14 = (bf16[1,2,32,1800]{3,2,1,0:T(8,128)(2,1)S(1)}, bf16[1,2,32,1800]{3,2,1,0:T(8,128)(2,1)S(1)}, u32[]{:S(2)}, u32[]{:S(2)}) collective-permute-start(bf16[1,2,32,1800]{3,2,1,0:T(8,128)(2,1)S(1)} %get-tuple-element.15), channel_id=1, source_target_pairs={{0,12},{4,8},{8,4},{12,0},{16,28},{20,24},{24,20},{28,16},{1,13},{... | collective-permute-start | bytes 691208 | tf_op jit(solution)/shard_map/ppermute | solution.py:31
  236.3 1.3 copy-start.3
